TPU v7x, 256 devices: a whole 4x4x8 slice. The times are simulated.
256 devices in a mesh: blk: 32 (over y, x, core), col: 8 (over z).
Axes of the slice: x: 4, y: 4, z: 8, core: 2. Of those that a mesh axis runs over, the one named last changes fastest.
Arguments:
- src_feat: bfloat16 [64, 1024, 256], P('blk', 'col'), may hold values from -40 to 40
- tgt_feat: bfloat16 [64, 1024, 256], P('blk', 'col'), may hold values from -40 to 40
- src_mass: bfloat16 [64, 1024], P('blk', 'col'), may hold values from 0.5 to 2
- tgt_mass: bfloat16 [64, 1024], P('blk', 'col'), may hold values from 0.5 to 2
- candidates: int32 [64, 8], P('blk'), may hold values from 0 to 63, as said below
- counts: int32 [64], P('blk'), may hold values from 1 to 8, as said below
- tgt_home: int32 [64], replicated, may hold values from 0 to 63, each once
Outputs:
- src_aligned: bfloat16 [64, 1024, 256], P('blk', 'col')
- tgt_aligned: bfloat16 [64, 1024, 256], P('blk', 'col')
Inputs may be any that keep to these rules, and one draw needn't show every extreme that they name: `candidates`: each row's 8 entries are distinct; the first counts[i] of row i are live, the others are not used; every target block number is among the live entries of some row. `counts`: the 2 blocks of one index of blk hold at most 12 live slots together, and the blocks of some index hold exactly 12. A permutation: target block number j is stored as block tgt_home[j] of tgt_feat and tgt_mass.
All inputs are finite; a program needn't handle non-finite values.
Results may differ from a plain program's by a relative error of at most 0.017.
Values may be sent and summed in bfloat16 or wider, within the bound.
No kernel may reach another device: no remote copies, remote signals or barrier semaphores. Data moves between devices by JAX's collectives and lax.ppermute only.
A program may use at most 64 MiB of HBM per device.

v0:
```python
import jax
import jax.numpy as jnp
from jax import lax
from jax.sharding import PartitionSpec as P

ITERS = 2
PAIRS = 12
score_offset = 0.3
softness_level = 0.02
epsilon = 1e-06
highest = lax.Precision.HIGHEST
slot_group = 4


def unit_rows(features):
    values = features.astype(jnp.float32)
    inverse = lax.rsqrt(jnp.mean(values * values, axis=-1, keepdims=True) + epsilon)
    return (values * inverse).astype(jnp.bfloat16)


def grouped(values_in):
    return values_in.reshape((values_in.shape[0] // slot_group, slot_group) + values_in.shape[1:])


def kernels(src_blocks, tgt_tiles):
    feature_total = src_blocks.shape[-1]
    score_matrix = jnp.einsum(
        "sbw,stw->sbt", src_blocks, tgt_tiles, preferred_element_type=jnp.float32
    )
    return jnp.exp((score_matrix / feature_total - score_offset) / softness_level)


def local(src_feat, tgt_feat, src_mass, tgt_mass, candidates, counts, tgt_home):
    local_blocks, sub_rows, feature_total = src_feat.shape
    slot_max = candidates.shape[1]
    block_count = tgt_home.shape[0]
    src_full, mass_full = (
        lax.all_gather(src_feat, "col", axis=1, tiled=True),
        lax.all_gather(src_mass, "col", axis=1, tiled=True),
    )
    full_rows = src_full.shape[1]
    src_unit = unit_rows(src_full)
    src_weight = mass_full.astype(jnp.float32)
    block_ids = jnp.arange(block_count, dtype=jnp.int32)
    local_ids = jnp.arange(local_blocks, dtype=jnp.int32)
    home_flat = jnp.sum(
        jnp.where(candidates.reshape(-1)[:, None] == block_ids[None, :], tgt_home[None, :], 0),
        axis=1,
    )
    slot_count = PAIRS
    block_ends = jnp.cumsum(counts)
    block_starts = block_ends - counts
    position = jnp.arange(slot_count, dtype=jnp.int32)
    src_of = jnp.minimum(
        jnp.sum((position[:, None] >= block_ends[None, :]).astype(jnp.int32), axis=1),
        local_blocks - 1,
    )
    owner_hot = src_of[:, None] == local_ids[None, :]
    within = position - jnp.sum(jnp.where(owner_hot, block_starts[None, :], 0), axis=1)
    alive_flag = position < block_ends[-1]
    flat_index = src_of * slot_max + jnp.clip(within, 0, slot_max - 1)
    flat_ids = jnp.arange(local_blocks * slot_max, dtype=jnp.int32)
    tgt_of = jnp.sum(
        jnp.where(flat_index[:, None] == flat_ids[None, :], home_flat[None, :], 0), axis=1
    )
    alive = alive_flag.astype(jnp.float32)
    masses = lax.all_gather(tgt_mass, "blk", axis=0, tiled=True).astype(jnp.float32)
    shard_piece = lax.all_gather(tgt_feat, "blk", axis=0, tiled=True)
    piece_rows = shard_piece.shape[0]
    chooser = (tgt_of[:, None] == jnp.arange(piece_rows, dtype=jnp.int32)[None, :]).astype(
        jnp.bfloat16
    )
    picked = jnp.einsum("sm,mtw->stw", chooser, shard_piece, preferred_element_type=jnp.float32)
    tiles_raw = picked.astype(jnp.bfloat16)
    tiles_unit = unit_rows(tiles_raw)
    pick_float = (tgt_of[:, None] == block_ids[None, :]).astype(jnp.float32)
    src_onehot = (src_of[:, None] == local_ids[None, :]).astype(jnp.float32)
    unit_groups = grouped(tiles_unit)
    raw_groups = grouped(tiles_raw)
    src_groups = grouped(src_of)
    active_group_flags = grouped(alive)
    group_indicator = grouped(src_onehot)
    kernel_elements = (unit_groups, src_groups)

    def tile_of(item):
        return kernels(jnp.take(src_unit, item[1], axis=0), item[0])

    def slot_scale_factors(column_scaling_vector):
        return grouped(
            jnp.einsum("sn,nt->st", pick_float, column_scaling_vector, precision=highest)
        )

    def row_pass(column_scaling_vector):

        def row_step(running, entry):
            item, alive_slots, onehot_slots, v_rows = entry
            kernel_tile = tile_of(item)
            row_part = (
                jnp.einsum("sbt,st->sb", kernel_tile, v_rows, precision=highest)
                * alive_slots[:, None]
            )
            return (
                running + jnp.einsum("sp,sb->pb", onehot_slots, row_part, precision=highest),
                None,
            )

        start_rows = jnp.zeros((local_blocks, full_rows), jnp.float32)
        result, _ = lax.scan(
            row_step,
            start_rows,
            (
                kernel_elements,
                active_group_flags,
                group_indicator,
                slot_scale_factors(column_scaling_vector),
            ),
        )
        return result

    def col_pass(scaling_u):

        def col_step(running, entry):
            item, src_ids, alive_slots = entry
            kernel_tile = tile_of(item)
            u_rows = jnp.take(scaling_u, src_ids, axis=0)
            col_part = (
                jnp.einsum("sb,sbt->st", u_rows, kernel_tile, precision=highest)
                * alive_slots[:, None]
            )
            return (running, col_part)

        _, col_parts = lax.scan(
            col_step, jnp.zeros((), jnp.float32), (kernel_elements, src_groups, active_group_flags)
        )
        return jnp.einsum(
            "sn,st->nt", pick_float, col_parts.reshape(slot_count, sub_rows), precision=highest
        )

    column_scaling_vector = jnp.ones((block_count, sub_rows), jnp.float32)
    scaling_u = jnp.ones((local_blocks, full_rows), jnp.float32)
    for iteration in range(ITERS):
        row_sums = lax.psum(row_pass(column_scaling_vector), "col")
        scaling_u = src_weight / row_sums
        col_terms = col_pass(scaling_u)
        column_scaling_vector = masses / lax.psum(col_terms.astype(jnp.bfloat16), "blk").astype(
            jnp.float32
        )

    def final_step(running, entry):
        item, raw_tiles, src_ids, alive_slots, onehot_slots, v_rows = entry
        kernel_tile = tile_of(item)
        u_rows = jnp.take(scaling_u, src_ids, axis=0)
        plan = (
            u_rows[:, :, None] * kernel_tile * v_rows[:, None, :] * alive_slots[:, None, None]
        ).astype(jnp.bfloat16)
        toward = jnp.einsum("sbt,stw->sbw", plan, raw_tiles, preferred_element_type=jnp.float32)
        running = running + jnp.einsum("sp,sbw->pbw", onehot_slots, toward, precision=highest)
        back_terms = jnp.einsum(
            "sbt,sbw->stw",
            plan,
            jnp.take(src_full, src_ids, axis=0),
            preferred_element_type=jnp.float32,
        )
        return (running, back_terms)

    start_sums = jnp.zeros((local_blocks, full_rows, feature_total), jnp.float32)
    final_entries = (
        kernel_elements,
        raw_groups,
        src_groups,
        active_group_flags,
        group_indicator,
        slot_scale_factors(column_scaling_vector),
    )
    src_sums, pair_sums = lax.scan(final_step, start_sums, final_entries)
    pair_sums = pair_sums.reshape(slot_count, sub_rows, feature_total)
    src_own = lax.psum_scatter(
        src_sums.astype(jnp.bfloat16), "col", scatter_dimension=1, tiled=True
    ).astype(jnp.float32)
    wanted = (
        jnp.arange(local_blocks * lax.axis_size("blk"), dtype=jnp.int32)[:, None] == tgt_of[None, :]
    ).astype(jnp.float32)
    tgt_own = lax.psum_scatter(
        jnp.einsum("ns,stw->ntw", wanted, pair_sums, precision=highest).astype(jnp.bfloat16),
        "blk",
        scatter_dimension=0,
        tiled=True,
    ).astype(jnp.float32)
    src_aligned = (src_own / src_mass.astype(jnp.float32)[:, :, None]).astype(jnp.bfloat16)
    tgt_aligned = (tgt_own / tgt_mass.astype(jnp.float32)[:, :, None]).astype(jnp.bfloat16)
    return (src_aligned, tgt_aligned)


def solution(mesh):
    in_specs = (
        P("blk", "col", None),
        P("blk", "col", None),
        P("blk", "col"),
        P("blk", "col"),
        P("blk", None),
        P("blk"),
        P(),
    )
    out_specs = (P("blk", "col", None), P("blk", "col", None))
    return jax.shard_map(local, mesh=mesh, in_specs=in_specs, out_specs=out_specs, check_vma=False)
```

profile of v0, /device:TPU:2, one launch (start us, length us, event | category | flops | bytes accessed | tf_op | source)
XLA Modules:
  0.0 660.9 jit_solution(15419486938049489401)
XLA Ops:
  13.0 19.3 %all_gather.12 = bf16[2,1024]{1,0:T(2,128)(2,1)S(1)} all-gather(bf16[2,128]{1,0:T(2,128)(2,1)} %param.23), channel_id=1, replica_groups=mesh['blk'=32,'col'=8] {'col'}, dimensions={1}, use_global_device_ids=true | all-gather | bytes 4608 | tf_op jit(solution)/shard_map/all_gather | solution.py:39
  32.3 21.5 %all-gather = bf16[32,2,128]{2,1,0:T(2,128)(2,1)S(1)} all-gather(bf16[1,2,128]{2,1,0:T(2,128)(2,1)} %bitcast.188), channel_id=1, replica_groups=mesh['blk'=32,'col'=8] {'blk'}, dimensions={0}, use_global_device_ids=true | all-gather | bytes 16896 | tf_op jit(solution)/shard_map/all_gather | solution.py:67
  54.7 1.6 fusion.129
  56.3 1.6 fusion.130
  57.9 45.0 %all-gather.6.cloned.1.call-done = bf16[64,128,256]{2,1,0:T(8,128)(2,1)} async-done(((bf16[2,128,256]{2,1,0:T(8,128)(2,1)}), bf16[64,128,256]{2,1,0:T(8,128)(2,1)}) %all-gather.6.cloned.1.call-update) | async-done | bytes 4194320 | tf_op jit(solution)/shard_map/all_gather | solution.py:68
  102.9 4.6 fusion.131
  110.5 14.7 %while.67 = (s32[]{:T(128)}, f32[2,1024]{1,0:T(2,128)S(1)}, f32[3,4,2]{1,2,0:T(2,128)S(1)}, s32[3,4]{1,0:T(4,128)S(1)}, bf16[2,1024,256]{2,1,0:T(8,128)(2,1)S(1)...) while((s32[]{:T(128)}, f32[2,1024]{1,0:T(2,128)S(1)}, ...), condition=%wide.region_8.10_spmd.clone, body=%wide.region_7.9_spmd.clone.sunk | while | flops 277455904 | bytes 10809075 | solution.py:108
  111.2 1.7 fusion.222
  112.9 2.2 fusion.223
  116.1 1.7 fusion.222
  117.9 2.2 fusion.223
  121.1 1.7 fusion.222
  122.8 2.2 fusion.223
  125.2 17.7 %psum.28 = f32[2,1024]{1,0:T(2,128)S(1)} all-reduce(f32[2,1024]{1,0:T(2,128)S(1)} %get-tuple-element.534), channel_id=1, replica_groups=mesh['blk'=32,'col'=8] {'col'}, use_global_device_ids=true, to_apply=%region_9.11 | all-reduce | flops 2048 | bytes 16384 | tf_op jit(solution)/shard_map/psum | solution.py:142
  143.0 13.8 %while.65 = (s32[]{:T(128)}, f32[3,4,128]{2,1,0:T(4,128)S(1)}, s32[3,4]{1,0:T(4,128)S(1)}, f32[2,1024]{1,0:T(2,128)S(1)}, bf16[2,1024,256]{2,1,0:T(8,128)(2,1)S(...) while((s32[]{:T(128)}, f32[3,4,128]{2,1,0:T(4,128)S(1)}, ...), condition=%wide.region_11.14_spmd, body=%wide.region_10.13_spmd.sunk | while | flops 277354016 | bytes 10840809 | solution.py:132
  144.4 1.7 fusion.207
  146.1 1.4 fusion.208
  149.0 1.7 fusion.207
  150.7 1.4 fusion.208
  153.6 1.7 fusion.207
  155.3 1.4 fusion.208
  157.2 119.3 %psum.29 = bf16[64,128]{1,0:T(8,128)(2,1)S(1)} all-reduce(bf16[64,128]{1,0:T(8,128)(2,1)S(1)} %convolution_convert_fusion.2), channel_id=1, replica_groups=mesh['blk'=32,'col'=8] {'blk'}, use_global_device_ids=true, to_apply=%region_12.15 | all-reduce | flops 8192 | bytes 32768 | tf_op jit(solution)/shard_map/psum | solution.py:145
  276.6 14.8 %while.68 = (s32[]{:T(128)}, f32[2,1024]{1,0:T(2,128)S(1)}, f32[3,4,2]{1,2,0:T(2,128)S(1)}, s32[3,4]{1,0:T(4,128)S(1)}, bf16[2,1024,256]{2,1,0:T(8,128)(2,1)S(1)...) while((s32[]{:T(128)}, f32[2,1024]{1,0:T(2,128)S(1)}, ...), condition=%wide.region_14.17_spmd.clone, body=%wide.region_13.16_spmd.clone.sunk | while | flops 277455904 | bytes 10809075 | solution.py:108
  277.4 1.7 fusion.230
  279.1 2.2 fusion.231
  282.3 1.7 fusion.230
  284.0 2.2 fusion.231
  287.2 1.7 fusion.230
  289.0 2.2 fusion.231
  291.4 15.3 %psum.30 = f32[2,1024]{1,0:T(2,128)S(1)} all-reduce(f32[2,1024]{1,0:T(2,128)S(1)} %get-tuple-element.536), channel_id=1, replica_groups=mesh['blk'=32,'col'=8] {'col'}, use_global_device_ids=true, to_apply=%region_15.18 | all-reduce | flops 2048 | bytes 16384 | tf_op jit(solution)/shard_map/psum | solution.py:142
  306.7 19.8 %while.66 = (s32[]{:T(128)}, f32[3,4,128]{2,1,0:T(4,128)S(1)}, s32[3,4]{1,0:T(4,128)S(1)}, f32[2,1024]{1,0:T(2,128)S(1)}, bf16[2,1024,256]{2,1,0:T(8,128)(2,1)S(...) while((s32[]{:T(128)}, f32[3,4,128]{2,1,0:T(4,128)S(1)}, ...), condition=%wide.region_17.20_spmd, body=%wide.region_16.19_spmd.sunk | while | flops 277354016 | bytes 10840809 | solution.py:132
  307.4 2.0 gather_fusion.2
  309.5 2.3 fusion.214
  311.8 1.4 fusion.215
  314.0 2.0 gather_fusion.2
  316.0 2.3 fusion.214
  318.4 1.4 fusion.215
  320.6 2.0 gather_fusion.2
  322.6 2.3 fusion.214
  325.0 1.4 fusion.215
  326.8 124.0 %psum.31 = bf16[64,128]{1,0:T(8,128)(2,1)S(1)} all-reduce(bf16[64,128]{1,0:T(8,128)(2,1)S(1)} %convolution_convert_fusion.1), channel_id=1, replica_groups=mesh['blk'=32,'col'=8] {'blk'}, use_global_device_ids=true, to_apply=%region_18.21 | all-reduce | flops 8192 | bytes 32768 | tf_op jit(solution)/shard_map/psum | solution.py:145
  451.1 68.1 %while.69 = (s32[]{:T(128)}, f32[2,1024,256]{2,0,1:T(2,128)}, f32[3,4,128,256]{3,2,1,0:T(8,128)}, f32[3,4,2]{1,2,0:T(2,128)S(1)}, s32[3,4]{1,0:T(4,128)S(1)}, /*...) while((s32[]{:T(128)}, f32[2,1024,256]{2,0,1:T(2,128)}, ...), condition=%wide.region_20.23_spmd.clone, body=%wide.region_19.22_spmd.clone.sunk | while | flops 837293056 | bytes 54619556 | solution.py:175
  451.8 2.0 gather_fusion.8
  453.8 2.0 gather_fusion.6
  455.8 2.7 multiply_convert_fusion.2
  459.9 1.8 fusion.242
  461.7 10.7 %select_add_fusion.2 = f32[2,1024,256]{2,0,1:T(2,128)S(1)} fusion(f32[2,1024,256]{2,0,1:T(2,128)S(1)} %copy-done.1, pred[]{:T(512)S(6)} %compare.11, f32[4,1024,256]{2,1,0:T(8,128)S(1)} %fusion.242, f32[3,4,2]{1,2,0:T(2,128)S(1)} %get-tuple-element.1191, s32[]{:T(128)S(6)} %copy.139), kind=kOutput, calls=%fused_computation.139.clone.1 | convolution fusion | flops 26214400 | bytes 8389637 | tf_op jit(solution)/shard_map/while/body/eval_jaxpr/sp,sbw->pbw/dot_general | solution.py:157
  474.5 2.0 gather_fusion.8
  476.5 2.0 gather_fusion.6
  478.5 2.7 multiply_convert_fusion.2
  482.7 1.8 fusion.242
  484.5 10.7 %select_add_fusion.2 = f32[2,1024,256]{2,0,1:T(2,128)S(1)} fusion(f32[2,1024,256]{2,0,1:T(2,128)S(1)} %copy-done.1, pred[]{:T(512)S(6)} %compare.11, f32[4,1024,256]{2,1,0:T(8,128)S(1)} %fusion.242, f32[3,4,2]{1,2,0:T(2,128)S(1)} %get-tuple-element.1191, s32[]{:T(128)S(6)} %copy.139), kind=kOutput, calls=%fused_computation.139.clone.1 | convolution fusion | flops 26214400 | bytes 8389637 | tf_op jit(solution)/shard_map/while/body/eval_jaxpr/sp,sbw->pbw/dot_general | solution.py:157
  497.2 2.0 gather_fusion.8
  499.2 2.0 gather_fusion.6
  501.2 2.7 multiply_convert_fusion.2
  505.3 1.8 fusion.242
  507.1 10.7 %select_add_fusion.2 = f32[2,1024,256]{2,0,1:T(2,128)S(1)} fusion(f32[2,1024,256]{2,0,1:T(2,128)S(1)} %copy-done.1, pred[]{:T(512)S(6)} %compare.11, f32[4,1024,256]{2,1,0:T(8,128)S(1)} %fusion.242, f32[3,4,2]{1,2,0:T(2,128)S(1)} %get-tuple-element.1191, s32[]{:T(128)S(6)} %copy.139), kind=kOutput, calls=%fused_computation.139.clone.1 | convolution fusion | flops 26214400 | bytes 8389637 | tf_op jit(solution)/shard_map/while/body/eval_jaxpr/sp,sbw->pbw/dot_general | solution.py:157
  519.2 2.9 copy.96
  522.4 4.0 convolution_convert_fusion
  526.4 4.3 copy.63
  531.5 29.2 %reduce-scatter.3.cloned.1.call-done = bf16[2,128,256]{2,1,0:T(8,128)(2,1)} async-done(((bf16[2,1024,256]{2,1,0:T(8,128)(2,1)}), bf16[2,128,256]{2,1,0:T(8,128)(2,1)}) %reduce-scatter.3.cloned.1.call-update) | async-done | bytes 131088 | tf_op jit(solution)/shard_map/reduce_scatter | solution.py:177
  560.6 1.7 divide_convert_fusion.1
  562.3 90.4 %reduce-scatter.5.cloned.1.call-done = bf16[2,128,256]{2,1,0:T(8,128)(2,1)} async-done(((bf16[64,128,256]{2,1,0:T(8,128)(2,1)}), bf16[2,128,256]{2,1,0:T(8,128)(2,1)}) %reduce-scatter.5.cloned.1.call-update) | async-done | bytes 131088 | tf_op jit(solution)/shard_map/reduce_scatter | solution.py:183
  652.7 1.7 divide_convert_fusion
  (171 shorter events, 34.2 us)
Async XLA Ops:
  7.2 47.5 %all-gather.4.cloned.1.call-start = ((), (), s32[]{:S(2)}) async-start(), calls=%async_computation.2 | async-start | bytes 1179648 | tf_op jit(solution)/shard_map/all_gather | solution.py:38
  7.9 95.0 %all-gather.6.cloned.1.call-start = ((), (), s32[]{:S(2)}) async-start(), calls=%async_computation.3 | async-start | bytes 4325376 | tf_op jit(solution)/shard_map/all_gather | solution.py:68
  8.6 552.0 %reduce-scatter.3.cloned.1.call-start = ((), (), s32[]{:S(2)}) async-start(), calls=%async_computation.4 | async-start | bytes 1179648 | tf_op jit(solution)/shard_map/reduce_scatter | solution.py:177
  306.7 144.4 %copy-start = (bf16[2,1024,256]{2,1,0:T(8,128)(2,1)S(1)}, bf16[2,1024,256]{2,1,0:T(8,128)(2,1)}, u32[]{:S(2)}) copy-start(bf16[2,1024,256]{2,1,0:T(8,128)(2,1)} %all-gather.4.cloned.1.call-done) | copy-start | bytes 3145732
  455.8 2.7 copy-start.3
  459.9 1.8 copy-start.1
  472.5 1.3 copy-start.2
  478.5 2.7 copy-start.3
  482.6 1.8 copy-start.1
  495.2 1.3 copy-start.2
  501.2 2.7 copy-start.3
  505.3 1.8 copy-start.1
  517.9 1.3 copy-start.2
  519.2 3.2 copy-start.4
  522.1 130.6 %reduce-scatter.5.cloned.1.call-start = ((), (), s32[]{:S(2)}) async-start(), calls=%async_computation.5 | async-start | bytes 4325376 | tf_op jit(solution)/shard_map/reduce_scatter | solution.py:183
  530.8 0.7 copy-start.5
  530.8 0.7 copy-start.6
Sparse Core Ops, SparseCore 0:
  9.8 41.3 all-gather.3
  53.7 49.1 all-gather.5
  522.2 38.3 reduce-scatter.2
  564.4 88.2 reduce-scatter.4
where the time goes:
time: 662 us; the launch traced here: 661 us
  blocking collectives  317 us (48%)
  waiting for transfers between devices  166 us (25%)
  matrix products  105 us (16%)
  local copies, waits for them, and re-layouts  45.6 us (7%)
  between operations  14 us (2%)
  other arithmetic  11.7 us (2%)
    psum x2, blocking collectives, local(): lax.psum(col_terms.astype(jnp.bfloat16), 'blk').astype(jnp.float32)  243 us
    reduce_scatter x1, waiting for transfers between devices, local(): lax.psum_scatter(jnp.einsum('ns,stw->ntw', wanted, pair_sums, precision=h...  90.4 us
    all_gather x1, waiting for transfers between devices, local(): shard_piece = lax.all_gather(tgt_feat, 'blk', axis=0, tiled=True)  45 us
    psum x2, blocking collectives, local(): row_sums = lax.psum(row_pass(column_scaling_vector), 'col')  33 us
    dot_general x3, matrix products, final_step(): jnp.einsum('sp,sbw->pbw', onehot_slots, toward, precision=highest)  32.2 us
    dot_general x15, matrix products, kernels(): jnp.einsum('sbw,stw->sbt', src_blocks, tgt_tiles, preferred_element_type=...  30.5 us
    reduce_scatter x1, waiting for transfers between devices, local(): lax.psum_scatter(src_sums.astype(jnp.bfloat16), 'col', scatter_dimension=...  29.2 us
    all_gather x1, blocking collectives, local(): lax.all_gather(tgt_mass, 'blk', axis=0, tiled=True).astype(jnp.float32)  21.5 us
  transfers between devices with their start and end apart: 4, of which 3 were waited for; matrix products, arithmetic and copies ran while one was open for 3% of the time, Pallas kernels for 0%

commit v1 on v0

--- a/solution.py
+++ b/solution.py
@@ -142,9 +142,9 @@
         row_sums = lax.psum(row_pass(column_scaling_vector), "col")
         scaling_u = src_weight / row_sums
         col_terms = col_pass(scaling_u)
-        column_scaling_vector = masses / lax.psum(col_terms.astype(jnp.bfloat16), "blk").astype(
-            jnp.float32
-        )
+        column_scaling_vector = masses / jnp.sum(
+            lax.all_gather(col_terms.astype(jnp.bfloat16), "blk"), axis=0
+        ).astype(jnp.float32)
 
     def final_step(running, entry):
         item, raw_tiles, src_ids, alive_slots, onehot_slots, v_rows = entry

time: 662 us -> 464 us (0.70)
  blocking collectives: 317 us -> 121 us
    psum x2 -> x0, blocking collectives: 243 us -> none  [local(): lax.psum(col_terms.astype(jnp.bfloat16), 'blk').astype(jnp.float32)]
    all_gather x0 -> x2, blocking collectives: none -> 47.1 us  [local(): lax.all_gather(col_terms.astype(jnp.bfloat16), 'blk')]
  transfers between devices with their start and end apart: 4 -> 4, of which waited for: 3 -> 3; matrix products, arithmetic and copies ran while one was open for 3% -> 4% of each run, Pallas kernels for 0% -> 0%
where the time goes in v1:
time: 464 us; the launch traced here: 463 us
  waiting for transfers between devices  164 us (35%)
  blocking collectives  121 us (26%)
  matrix products  105 us (23%)
  local copies, waits for them, and re-layouts  45.6 us (10%)
  between operations  14 us (3%)
  other arithmetic  11.9 us (3%)
    reduce_scatter x1, waiting for transfers between devices, local(): lax.psum_scatter(jnp.einsum('ns,stw->ntw', wanted, pair_sums, precision=h...  90.5 us
    all_gather x2, blocking collectives, local(): lax.all_gather(col_terms.astype(jnp.bfloat16), 'blk')  47.1 us
    all_gather x1, waiting for transfers between devices, local(): shard_piece = lax.all_gather(tgt_feat, 'blk', axis=0, tiled=True)  45 us
    psum x2, blocking collectives, local(): row_sums = lax.psum(row_pass(column_scaling_vector), 'col')  33 us
    dot_general x3, matrix products, final_step(): jnp.einsum('sp,sbw->pbw', onehot_slots, toward, precision=highest)  32.2 us
    dot_general x15, matrix products, kernels(): jnp.einsum('sbw,stw->sbt', src_blocks, tgt_tiles, preferred_element_type=...  30.5 us
    reduce_scatter x1, waiting for transfers between devices, local(): lax.psum_scatter(src_sums.astype(jnp.bfloat16), 'col', scatter_dimension=...  27.2 us
    all_gather x1, blocking collectives, local(): lax.all_gather(tgt_mass, 'blk', axis=0, tiled=True).astype(jnp.float32)  21.5 us
  transfers between devices with their start and end apart: 4, of which 3 were waited for; matrix products, arithmetic and copies ran while one was open for 4% of the time, Pallas kernels for 0%

profile of v1, /device:TPU:2, one launch (start us, length us, event | category | flops | bytes accessed | tf_op | source)
XLA Modules:
  0.0 463.0 jit_solution(6371550108253398680)
XLA Ops:
  13.0 19.3 %all_gather.24 = bf16[2,1024]{1,0:T(2,128)(2,1)S(1)} all-gather(bf16[2,128]{1,0:T(2,128)(2,1)} %param.23), channel_id=1, replica_groups=mesh['blk'=32,'col'=8] {'col'}, dimensions={1}, use_global_device_ids=true | all-gather | bytes 4608 | tf_op jit(solution)/shard_map/all_gather | solution.py:39
  32.3 21.5 %all-gather.2 = bf16[32,2,128]{2,1,0:T(2,128)(2,1)S(1)} all-gather(bf16[1,2,128]{2,1,0:T(2,128)(2,1)} %bitcast.192), channel_id=1, replica_groups=mesh['blk'=32,'col'=8] {'blk'}, dimensions={0}, use_global_device_ids=true | all-gather | bytes 16896 | tf_op jit(solution)/shard_map/all_gather | solution.py:67
  54.7 1.6 fusion.129
  56.3 1.6 fusion.130
  57.9 45.0 %all-gather.8.cloned.1.call-done = bf16[64,128,256]{2,1,0:T(8,128)(2,1)} async-done(((bf16[2,128,256]{2,1,0:T(8,128)(2,1)}), bf16[64,128,256]{2,1,0:T(8,128)(2,1)}) %all-gather.8.cloned.1.call-update) | async-done | bytes 4194320 | tf_op jit(solution)/shard_map/all_gather | solution.py:68
  102.9 4.6 %fusion.131 = (f32[12,128]{0,1:T(8,128)S(1)}, bf16[12,128,256]{2,0,1:T(8,128)(2,1)S(1)}) fusion(bf16[64,128,256]{2,1,0:T(8,128)(2,1)} %all-gather.8.cloned.1.call-done, s32[12]{0:T(128)S(1)} %select_reduce_fusion), kind=kOutput, calls=%fused_computation.176 | convolution fusion | flops 51903744 | bytes 4986928 | tf_op jit(solution)/shard_map/sm,mtw->stw/dot_general | solution.py:73
  110.5 14.7 %while.67 = (s32[]{:T(128)}, f32[2,1024]{1,0:T(2,128)S(1)}, f32[3,4,2]{1,2,0:T(2,128)S(1)}, s32[3,4]{1,0:T(4,128)S(1)}, bf16[2,1024,256]{2,1,0:T(8,128)(2,1)S(1)...) while((s32[]{:T(128)}, f32[2,1024]{1,0:T(2,128)S(1)}, ...), condition=%wide.region_8.10_spmd.clone, body=%wide.region_7.9_spmd.clone.sunk | while | flops 277455904 | bytes 10809075 | solution.py:108
  111.2 1.7 fusion.222
  112.9 2.2 fusion.223
  116.1 1.7 fusion.222
  117.9 2.2 fusion.223
  121.1 1.7 fusion.222
  122.8 2.2 fusion.223
  125.2 17.7 %psum.14 = f32[2,1024]{1,0:T(2,128)S(1)} all-reduce(f32[2,1024]{1,0:T(2,128)S(1)} %get-tuple-element.534), channel_id=1, replica_groups=mesh['blk'=32,'col'=8] {'col'}, use_global_device_ids=true, to_apply=%region_9.11 | all-reduce | flops 2048 | bytes 16384 | tf_op jit(solution)/shard_map/psum | solution.py:142
  143.0 13.8 %while.65 = (s32[]{:T(128)}, f32[3,4,128]{2,1,0:T(4,128)S(1)}, s32[3,4]{1,0:T(4,128)S(1)}, f32[2,1024]{1,0:T(2,128)S(1)}, bf16[2,1024,256]{2,1,0:T(8,128)(2,1)S(...) while((s32[]{:T(128)}, f32[3,4,128]{2,1,0:T(4,128)S(1)}, ...), condition=%wide.region_11.14_spmd, body=%wide.region_10.13_spmd.sunk | while | flops 277354016 | bytes 10840809 | solution.py:132
  144.4 1.7 fusion.207
  146.1 1.4 fusion.208
  149.0 1.7 fusion.207
  150.7 1.4 fusion.208
  153.6 1.7 fusion.207
  155.3 1.4 fusion.208
  157.2 23.3 %all-gather = bf16[2048,128]{1,0:T(8,128)(2,1)S(1)} all-gather(bf16[64,128]{1,0:T(8,128)(2,1)S(1)} %convolution_convert_fusion.2), channel_id=2, replica_groups=mesh['blk'=32,'col'=8] {'blk'}, dimensions={0}, use_global_device_ids=true | all-gather | bytes 540672 | tf_op jit(solution)/shard_map/all_gather | solution.py:146
  180.8 14.8 %while.68 = (s32[]{:T(128)}, f32[2,1024]{1,0:T(2,128)S(1)}, f32[3,4,2]{1,2,0:T(2,128)S(1)}, s32[3,4]{1,0:T(4,128)S(1)}, bf16[2,1024,256]{2,1,0:T(8,128)(2,1)S(1)...) while((s32[]{:T(128)}, f32[2,1024]{1,0:T(2,128)S(1)}, ...), condition=%wide.region_14.17_spmd.clone, body=%wide.region_13.16_spmd.clone.sunk | while | flops 277455904 | bytes 10809075 | solution.py:108
  181.6 1.7 fusion.230
  183.3 2.2 fusion.231
  186.5 1.7 fusion.230
  188.2 2.2 fusion.231
  191.4 1.7 fusion.230
  193.1 2.2 fusion.231
  195.6 15.3 %psum.15 = f32[2,1024]{1,0:T(2,128)S(1)} all-reduce(f32[2,1024]{1,0:T(2,128)S(1)} %get-tuple-element.536), channel_id=1, replica_groups=mesh['blk'=32,'col'=8] {'col'}, use_global_device_ids=true, to_apply=%region_15.18 | all-reduce | flops 2048 | bytes 16384 | tf_op jit(solution)/shard_map/psum | solution.py:142
  210.9 19.8 %while.66 = (s32[]{:T(128)}, f32[3,4,128]{2,1,0:T(4,128)S(1)}, s32[3,4]{1,0:T(4,128)S(1)}, f32[2,1024]{1,0:T(2,128)S(1)}, bf16[2,1024,256]{2,1,0:T(8,128)(2,1)S(...) while((s32[]{:T(128)}, f32[3,4,128]{2,1,0:T(4,128)S(1)}, ...), condition=%wide.region_17.20_spmd, body=%wide.region_16.19_spmd.sunk | while | flops 277354016 | bytes 10840809 | solution.py:132
  211.6 2.0 gather_fusion.2
  213.6 2.3 fusion.214
  216.0 1.4 fusion.215
  218.2 2.0 gather_fusion.2
  220.2 2.3 fusion.214
  222.5 1.4 fusion.215
  224.8 2.0 gather_fusion.2
  226.8 2.3 fusion.214
  229.1 1.4 fusion.215
  231.0 23.8 %all-gather.1 = bf16[2048,128]{1,0:T(8,128)(2,1)S(1)} all-gather(bf16[64,128]{1,0:T(8,128)(2,1)S(1)} %convolution_convert_fusion.1), channel_id=3, replica_groups=mesh['blk'=32,'col'=8] {'blk'}, dimensions={0}, use_global_device_ids=true | all-gather | bytes 540672 | tf_op jit(solution)/shard_map/all_gather | solution.py:146
  255.0 68.1 %while.69 = (s32[]{:T(128)}, f32[2,1024,256]{2,0,1:T(2,128)}, f32[3,4,128,256]{3,2,1,0:T(8,128)}, f32[3,4,2]{1,2,0:T(2,128)S(1)}, s32[3,4]{1,0:T(4,128)S(1)}, /*...) while((s32[]{:T(128)}, f32[2,1024,256]{2,0,1:T(2,128)}, ...), condition=%wide.region_20.23_spmd.clone, body=%wide.region_19.22_spmd.clone.sunk | while | flops 837293056 | bytes 54619556 | solution.py:175
  255.8 2.0 gather_fusion.8
  257.8 2.0 gather_fusion.6
  259.8 2.7 multiply_convert_fusion.2
  263.9 1.8 fusion.242
  265.7 10.7 %select_add_fusion.2 = f32[2,1024,256]{2,0,1:T(2,128)S(1)} fusion(f32[2,1024,256]{2,0,1:T(2,128)S(1)} %copy-done.1, pred[]{:T(512)S(6)} %compare.11, f32[4,1024,256]{2,1,0:T(8,128)S(1)} %fusion.242, f32[3,4,2]{1,2,0:T(2,128)S(1)} %get-tuple-element.1191, s32[]{:T(128)S(6)} %copy.139), kind=kOutput, calls=%fused_computation.139.clone.1 | convolution fusion | flops 26214400 | bytes 8389637 | tf_op jit(solution)/shard_map/while/body/eval_jaxpr/sp,sbw->pbw/dot_general | solution.py:157
  278.5 2.0 gather_fusion.8
  280.5 2.0 gather_fusion.6
  282.5 2.7 multiply_convert_fusion.2
  286.6 1.8 fusion.242
  288.4 10.7 %select_add_fusion.2 = f32[2,1024,256]{2,0,1:T(2,128)S(1)} fusion(f32[2,1024,256]{2,0,1:T(2,128)S(1)} %copy-done.1, pred[]{:T(512)S(6)} %compare.11, f32[4,1024,256]{2,1,0:T(8,128)S(1)} %fusion.242, f32[3,4,2]{1,2,0:T(2,128)S(1)} %get-tuple-element.1191, s32[]{:T(128)S(6)} %copy.139), kind=kOutput, calls=%fused_computation.139.clone.1 | convolution fusion | flops 26214400 | bytes 8389637 | tf_op jit(solution)/shard_map/while/body/eval_jaxpr/sp,sbw->pbw/dot_general | solution.py:157
  301.2 2.0 gather_fusion.8
  303.2 2.0 gather_fusion.6
  305.2 2.7 multiply_convert_fusion.2
  309.3 1.8 fusion.242
  311.1 10.7 %select_add_fusion.2 = f32[2,1024,256]{2,0,1:T(2,128)S(1)} fusion(f32[2,1024,256]{2,0,1:T(2,128)S(1)} %copy-done.1, pred[]{:T(512)S(6)} %compare.11, f32[4,1024,256]{2,1,0:T(8,128)S(1)} %fusion.242, f32[3,4,2]{1,2,0:T(2,128)S(1)} %get-tuple-element.1191, s32[]{:T(128)S(6)} %copy.139), kind=kOutput, calls=%fused_computation.139.clone.1 | convolution fusion | flops 26214400 | bytes 8389637 | tf_op jit(solution)/shard_map/while/body/eval_jaxpr/sp,sbw->pbw/dot_general | solution.py:157
  323.2 2.9 copy.96
  326.4 4.0 convolution_convert_fusion
  330.4 4.3 copy.63
  335.4 27.2 %reduce-scatter.3.cloned.1.call-done = bf16[2,128,256]{2,1,0:T(8,128)(2,1)} async-done(((bf16[2,1024,256]{2,1,0:T(8,128)(2,1)}), bf16[2,128,256]{2,1,0:T(8,128)(2,1)}) %reduce-scatter.3.cloned.1.call-update) | async-done | bytes 131088 | tf_op jit(solution)/shard_map/reduce_scatter | solution.py:177
  362.6 1.7 divide_convert_fusion.1
  364.3 90.5 %reduce-scatter.5.cloned.1.call-done = bf16[2,128,256]{2,1,0:T(8,128)(2,1)} async-done(((bf16[64,128,256]{2,1,0:T(8,128)(2,1)}), bf16[2,128,256]{2,1,0:T(8,128)(2,1)}) %reduce-scatter.5.cloned.1.call-update) | async-done | bytes 131088 | tf_op jit(solution)/shard_map/reduce_scatter | solution.py:183
  454.8 1.7 divide_convert_fusion
  (173 shorter events, 34.4 us)
Async XLA Ops:
  7.2 47.5 %all-gather.6.cloned.1.call-start = ((), (), s32[]{:S(2)}) async-start(), calls=%async_computation.2 | async-start | bytes 1179648 | tf_op jit(solution)/shard_map/all_gather | solution.py:38
  7.9 95.0 %all-gather.8.cloned.1.call-start = ((), (), s32[]{:S(2)}) async-start(), calls=%async_computation.3 | async-start | bytes 4325376 | tf_op jit(solution)/shard_map/all_gather | solution.py:68
  8.6 354.0 %reduce-scatter.3.cloned.1.call-start = ((), (), s32[]{:S(2)}) async-start(), calls=%async_computation.4 | async-start | bytes 1179648 | tf_op jit(solution)/shard_map/reduce_scatter | solution.py:177
  210.9 44.2 %copy-start = (bf16[2,1024,256]{2,1,0:T(8,128)(2,1)S(1)}, bf16[2,1024,256]{2,1,0:T(8,128)(2,1)}, u32[]{:S(2)}) copy-start(bf16[2,1024,256]{2,1,0:T(8,128)(2,1)} %all-gather.6.cloned.1.call-done) | copy-start | bytes 3145732
  259.8 2.7 copy-start.3
  263.9 1.8 copy-start.1
  276.5 1.3 copy-start.2
  282.5 2.7 copy-start.3
  286.6 1.8 copy-start.1
  299.2 1.3 copy-start.2
  305.2 2.7 copy-start.3
  309.3 1.8 copy-start.1
  321.8 1.3 copy-start.2
  323.2 3.2 copy-start.4
  326.1 128.7 %reduce-scatter.5.cloned.1.call-start = ((), (), s32[]{:S(2)}) async-start(), calls=%async_computation.5 | async-start | bytes 4325376 | tf_op jit(solution)/shard_map/reduce_scatter | solution.py:183
  334.8 0.7 copy-start.5
  334.8 0.7 copy-start.6
Sparse Core Ops, SparseCore 0:
  9.8 41.3 all-gather.5
  53.7 49.1 all-gather.7
  326.2 36.3 reduce-scatter.2
  366.4 88.3 reduce-scatter.4
